TPU v7x, 32 devices: a whole 2x2x4 slice. The times are simulated.
32 devices in a mesh: dom: 2 (over x), tok: 16 (over z, y, core).
Axes of the slice: x: 2, y: 2, z: 4, core: 2. Of those that a mesh axis runs over, the one named last changes fastest.
Arguments:
- tokens: bfloat16 [512, 4096], P(('dom', 'tok')), parts along dimension 0, may hold values from -6 to 6
- rotation_flip: int32 [4096], replicated, may hold values from 0 to 1
- gate_up: bfloat16 [4, 4096, 16384], P('dom', None, 'tok'), parts along dimension 0, may hold values from -0.09375 to 0.09375
- quant_codes: bfloat16 [4, 4096, 16384], P('dom', None, 'tok'), parts along dimension 0, may hold values from -7 to 7
- quant_exps: int32 [4, 32, 16384], P('dom', None, 'tok'), parts along dimension 0, may hold values from -10 to -7
- down_rows: bfloat16 [32768, 4096], P(('dom', 'tok')), parts along dimension 0, may hold values from -0.046875 to 0.046875
Outputs:
- correction: bfloat16 [32768, 4096], P(('dom', 'tok')), parts along dimension 0
There are 2 independent parts, one for each index of `dom`. A program takes and returns all parts, laid end to end along the dimension named above; an argument that names none is the same for every part. Nothing has to cross between parts.
All inputs are finite; a program needn't handle non-finite values.
Results may differ from a plain program's by a relative error of at most 0.012.
Values may be sent and summed in bfloat16 or wider, within the bound.
No kernel may reach another device: no remote copies, remote signals or barrier semaphores. Data moves between devices by JAX's collectives and lax.ppermute only.
A program may use at most 128 MiB of HBM per device.

v0:
```python
import jax
import jax.numpy as jnp
from jax import lax
from jax.sharding import PartitionSpec as P


def hadamard_table(order):
    index = jnp.arange(order, dtype=jnp.int32)
    common = index[:, None] & index[None, :]
    parity = jnp.zeros((order, order), jnp.int32)
    for bit_pos in range(max(order.bit_length() - 1, 1)):
        parity = parity ^ common >> bit_pos & 1
    return (1 - 2 * parity).astype(jnp.float32)


def rotate(inputs, flip):
    width = inputs.shape[-1]
    signed = inputs.astype(jnp.float32) * (1 - 2 * flip).astype(jnp.float32)
    power = width.bit_length() - 1
    outer_len = 2 ** (power // 2)
    inner_len = width // outer_len
    blocks = signed.reshape(-1, outer_len, inner_len)
    mixed = jnp.einsum(
        "ab,nbc,cd->nad",
        hadamard_table(outer_len),
        blocks,
        hadamard_table(inner_len),
        precision=lax.Precision.HIGHEST,
    )
    return (mixed.reshape(-1, width) * (1.0 / width**0.5)).astype(jnp.bfloat16)


def dequant(codes, exps):
    groups = exps.shape[1]
    scales = jnp.exp2(exps.astype(jnp.float32))
    shaped = codes.astype(jnp.float32).reshape(2, groups, codes.shape[1] // groups, codes.shape[2])
    return (shaped * scales[:, :, None, :]).reshape(codes.shape).astype(jnp.bfloat16)


def swiglu(inputs, weights):
    gate = jnp.dot(inputs, weights[0], preferred_element_type=jnp.float32)
    upper = jnp.dot(inputs, weights[1], preferred_element_type=jnp.float32)
    return (jax.nn.silu(gate) * upper).astype(jnp.bfloat16)


def per_device(tokens, rotation_flip, gate_up, quant_codes, quant_exps, down_rows):
    quant_weight = dequant(quant_codes, quant_exps)
    piece = lax.all_gather(tokens, "tok", axis=0, tiled=True)
    hid_full = swiglu(piece, gate_up)
    hid_quant = swiglu(rotate(piece, rotation_flip), quant_weight)
    mismatch = (hid_full.astype(jnp.float32) - hid_quant.astype(jnp.float32)).astype(jnp.bfloat16)
    total_tokens = mismatch.shape[0]
    partial_proj = jnp.dot(mismatch, down_rows, preferred_element_type=jnp.float32)
    projected = lax.psum(partial_proj, "tok").astype(jnp.bfloat16)
    gram = lax.dot_general(
        hid_quant, projected, (((0,), (0,)), ((), ())), preferred_element_type=jnp.float32
    )
    return (gram * (1.0 / total_tokens**0.5)).astype(jnp.bfloat16)


def solution(mesh):
    placed = (
        P(("dom", "tok"), None),
        P(),
        P("dom", None, "tok"),
        P("dom", None, "tok"),
        P("dom", None, "tok"),
        P(("dom", "tok"), None),
    )
    return jax.shard_map(
        per_device, mesh=mesh, in_specs=placed, out_specs=P(("dom", "tok"), None), check_vma=False
    )
```

profile of v0, /device:TPU:1, one launch (start us, length us, event | category | flops | bytes accessed | tf_op | source)
XLA Modules:
  0.0 203.8 jit_solution(15538142856855820026)
XLA Ops:
  6.5 0.0 all-gather.2.cloned.1.call-start
  6.5 0.7 all-gather.2.cloned.1.call-update
  7.3 1.0 multiply_exponential_fusion
  8.3 0.0 copy-start.2
  8.3 14.8 %fusion = bf16[2,4096,1024]{2,1,0:T(8,128)(2,1)} fusion(bf16[2,4096,1024]{2,1,0:T(8,128)(2,1)} %param.9, f32[2,32,1024]{2,1,0:T(8,128)S(1)} %multiply_exponential_fusion), kind=kLoop, calls=%fused_computation.1 | loop fusion | flops 25165824 | bytes 33816576 | tf_op jit(solution)/shard_map/convert_element_type | solution.py:37
  23.1 0.0 copy-done.2
  23.1 30.4 %all-gather.2.cloned.1.call-done = bf16[256,4096]{1,0:T(8,128)(2,1)} async-done(((bf16[16,4096]{1,0:T(8,128)(2,1)}), bf16[256,4096]{1,0:T(8,128)(2,1)}) %all-gather.2.cloned.1.call-update) | async-done | bytes 2097168 | tf_op jit(solution)/shard_map/all_gather | solution.py:48
  53.4 3.3 %copy.8 = bf16[256,4096]{0,1:T(8,128)(2,1)S(1)} copy(bf16[256,4096]{1,0:T(8,128)(2,1)} %all-gather.2.cloned.1.call-done) | data formatting | bytes 4194304 | tf_op jit(solution)/shard_map/all_gather | solution.py:48
  56.7 0.0 copy-start
  56.7 0.7 convert_multiply_fusion
  57.5 6.8 %fusion.11 = f32[256,64,64]{0,2,1:T(8,128)S(1)} fusion(f32[256,64,64]{0,2,1:T(8,128)S(1)} %bitcast.47), kind=kOutput, calls=%fused_computation.15 | convolution fusion | flops 805392384 | bytes 8388608 | tf_op jit(solution)/shard_map/ab,nbc,cd->nad/dot_general | solution.py:23
  64.2 6.0 %multiply_convert_fusion.1 = bf16[256,64,64]{0,2,1:T(8,128)(2,1)S(1)} fusion(f32[256,64,64]{0,2,1:T(8,128)S(1)} %fusion.11), kind=kOutput, calls=%fused_computation.17 | convolution fusion | flops 807489536 | bytes 6291456 | tf_op jit(solution)/shard_map/ab,nbc,cd->nad/dot_general | solution.py:23
  70.3 0.0 copy-done
  70.3 2.4 %fusion.2 = f32[256,1024]{1,0:T(8,128)S(1)} fusion(bf16[256,4096]{0,1:T(8,128)(2,1)S(1)} %bitcast.48, bf16[2,4096,1024]{2,1,0:T(8,128)(2,1)S(1)} %copy-done), kind=kOutput, calls=%fused_computation.6 | convolution fusion | flops 2147483648 | bytes 11534336 | tf_op jit(solution)/shard_map/dot_general | solution.py:41
  72.6 0.0 copy-start.1
  72.6 2.4 %fusion.20 = bf16[256,1024]{1,0:T(8,128)(2,1)S(1)} fusion(bf16[256,4096]{0,1:T(8,128)(2,1)S(1)} %bitcast.49, bf16[2,4096,1024]{2,1,0:T(8,128)(2,1)S(1)} %copy-done, f32[256,1024]{1,0:T(8,128)S(1)} %fusion.2), kind=kOutput, calls=%fused_computation.22 | convolution fusion | flops 2149056512 | bytes 12058624 | tf_op jit(solution)/shard_map/dot_general | solution.py:42
  75.1 0.0 copy-done.1
  75.1 6.7 %fusion.5 = f32[256,1024]{1,0:T(8,128)} fusion(bf16[256,4096]{1,0:T(8,128)(2,1)S(1)} %copy-done.1, bf16[2,4096,1024]{2,1,0:T(8,128)(2,1)} %param.8), kind=kOutput, calls=%fused_computation.9 | convolution fusion | flops 2147483648 | bytes 11534336 | tf_op jit(solution)/shard_map/dot_general | solution.py:41
  81.8 12.7 %fusion.34 = f32[256,4096]{1,0:T(8,128)} fusion(bf16[1024,4096]{1,0:T(8,128)(2,1)} %param.11, bf16[256,4096]{1,0:T(8,128)(2,1)S(1)} %copy-done.1, bf16[2,4096,1024]{2,1,0:T(8,128)(2,1)} %param.8, bf16[256,1024]{1,0:T(8,128)(2,1)S(1)} %fusion.20, f32[256,1024]{1,0:T(8,128)} %fusion.5), kind=kOutput, calls=%fused_computation.27 | convolution fusion | flops 4297588736 | bytes 24641536 | tf_op jit(solution)/shard_map/dot_general | solution.py:53
  94.5 96.6 %all-reduce.1 = bf16[256,4096]{1,0:T(8,128)(2,1)S(1)} all-reduce(f32[256,4096]{1,0:T(8,128)} %fusion.34), channel_id=1, replica_groups=mesh['dom'=2,'tok'=16] {'tok'}, use_global_device_ids=true, to_apply=%region_0.1 | all-reduce | flops 1048576 | bytes 6291456 | tf_op jit(solution)/shard_map/psum | solution.py:54
  191.1 5.8 %multiply_convert_fusion = bf16[1024,4096]{1,0:T(8,128)(2,1)} fusion(bf16[256,1024]{1,0:T(8,128)(2,1)S(1)} %fusion.20, bf16[256,4096]{1,0:T(8,128)(2,1)S(1)} %all-reduce.1), kind=kOutput, calls=%fused_computation.2 | convolution fusion | flops 2155872256 | bytes 11010048 | tf_op jit(solution)/shard_map/dot_general | solution.py:55
  (1 shorter events, 0.0 us)
Async XLA Ops:
  6.5 46.9 %all-gather.2.cloned.1.call-start = ((), (), s32[]{:S(2)}) async-start(), calls=%async_computation | async-start | bytes 2228224 | tf_op jit(solution)/shard_map/all_gather | solution.py:48
  8.3 14.8 %copy-start.2 = (s32[4096]{0:T(1024)S(1)}, s32[4096]{0:T(1024)}, u32[]{:S(2)}) copy-start(s32[4096]{0:T(1024)} %param.7) | copy-start | bytes 49156
  56.7 13.6 %copy-start = (bf16[2,4096,1024]{2,1,0:T(8,128)(2,1)S(1)}, bf16[2,4096,1024]{2,1,0:T(8,128)(2,1)}, u32[]{:S(2)}) copy-start(bf16[2,4096,1024]{2,1,0:T(8,128)(2,1)} %fusion) | copy-start | bytes 50331652
  72.6 2.5 %copy-start.1 = (bf16[256,4096]{1,0:T(8,128)(2,1)S(1)}, bf16[256,4096]{1,0:T(8,128)(2,1)}, u32[]{:S(2)}) copy-start(bf16[256,4096]{1,0:T(8,128)(2,1)} %all-gather.2.cloned.1.call-done) | copy-start | bytes 6291460
Sparse Core Ops, SparseCore 0:
  9.5 43.9 all-gather.1
where the time goes:
time: 204 us
  blocking collectives  96.6 us (47%)
  matrix products  42.8 us (21%)
  waiting for transfers between devices  31.1 us (15%)
  other arithmetic  16.5 us (8%)
  between operations  13.5 us (7%)
  local copies, waits for them, and re-layouts  3.28 us (2%)
    psum x1, blocking collectives, per_device(): projected = lax.psum(partial_proj, 'tok').astype(jnp.bfloat16)  96.6 us
    all_gather x1, waiting for transfers between devices, per_device(): piece = lax.all_gather(tokens, 'tok', axis=0, tiled=True)  30.4 us
    convert_element_type x1, other arithmetic, dequant(): (shaped * scales[:, :, None, :]).reshape(codes.shape).astype(jnp.bfloat16)  14.8 us
    dot_general x2, matrix products, rotate(): jnp.einsum('ab,nbc,cd->nad', hadamard_table(outer_len), blocks, hadamard_...  12.8 us
    dot_general x1, matrix products, per_device(): jnp.dot(mismatch, down_rows, preferred_element_type=jnp.float32)  12.7 us
    dot_general x2, matrix products, swiglu(): gate = jnp.dot(inputs, weights[0], preferred_element_type=jnp.float32)  9.03 us
    dot_general x1, matrix products, per_device(): lax.dot_general(hid_quant, projected, (((0,), (0,)), ((), ())), preferred...  5.79 us
  transfers between devices with their start and end apart: 1, of which 1 were waited for; matrix products, arithmetic and copies ran while one was open for 8% of the time, Pallas kernels for 0%

commit v1 on v0

--- a/solution.py
+++ b/solution.py
@@ -2,6 +2,7 @@
 import jax.numpy as jnp
 from jax import lax
 from jax.sharding import PartitionSpec as P
+from jax.lax import all_gather
 
 
 def hadamard_table(order):
@@ -51,7 +52,8 @@
     mismatch = (hid_full.astype(jnp.float32) - hid_quant.astype(jnp.float32)).astype(jnp.bfloat16)
     total_tokens = mismatch.shape[0]
     partial_proj = jnp.dot(mismatch, down_rows, preferred_element_type=jnp.float32)
-    projected = lax.psum(partial_proj, "tok").astype(jnp.bfloat16)
+    return_all_tiles = lambda array_here: jnp.sum(all_gather(array_here, axis_name="tok"), axis=0)
+    projected = return_all_tiles(partial_proj).astype(jnp.bfloat16)
     gram = lax.dot_general(
         hid_quant, projected, (((0,), (0,)), ((), ())), preferred_element_type=jnp.float32
     )

time: 204 us -> 454 us (2.23)
  waiting for transfers between devices: 31.1 us -> 356 us
  blocking collectives: 96.6 us -> 0 us
  other arithmetic: 16.5 us -> 37.8 us
    all_gather x0 -> x1, waiting for transfers between devices: none -> 325 us  [per_device(): all_gather(array_here, axis_name='tok')]
    psum x1 -> x0, blocking collectives: 96.6 us -> none  [per_device(): projected = lax.psum(partial_proj, 'tok').astype(jnp.bfloat16)]
    reduce_sum x0 -> x1, other arithmetic: none -> 21.3 us  [per_device(): jnp.sum(all_gather(array_here, axis_name='tok'), axis=0)]
  transfers between devices with their start and end apart: 1 -> 2, of which waited for: 1 -> 2; matrix products, arithmetic and copies ran while one was open for 8% -> 3% of each run, Pallas kernels for 0% -> 0%
where the time goes in v1:
time: 454 us; the launch traced here: 453 us
  waiting for transfers between devices  356 us (78%)
  matrix products  42.8 us (9%)
  other arithmetic  37.8 us (8%)
  between operations  13.5 us (3%)
    all_gather x1, waiting for transfers between devices, per_device(): all_gather(array_here, axis_name='tok')  325 us
    all_gather x1, waiting for transfers between devices, per_device(): piece = lax.all_gather(tokens, 'tok', axis=0, tiled=True)  30.4 us
    reduce_sum x1, other arithmetic, per_device(): jnp.sum(all_gather(array_here, axis_name='tok'), axis=0)  21.3 us
    convert_element_type x1, other arithmetic, dequant(): (shaped * scales[:, :, None, :]).reshape(codes.shape).astype(jnp.bfloat16)  14.8 us
    dot_general x2, matrix products, rotate(): jnp.einsum('ab,nbc,cd->nad', hadamard_table(outer_len), blocks, hadamard_...  12.8 us
    dot_general x1, matrix products, per_device(): jnp.dot(mismatch, down_rows, preferred_element_type=jnp.float32)  12.7 us
  transfers between devices with their start and end apart: 2, of which 2 were waited for; matrix products, arithmetic and copies ran while one was open for 3% of the time, Pallas kernels for 0%

profile of v1, /device:TPU:1, one launch (start us, length us, event | category | flops | bytes accessed | tf_op | source)
XLA Modules:
  0.0 453.5 jit_solution(15188079136583211345)
XLA Ops:
  6.5 0.0 all-gather.4.cloned.1.call-start
  6.5 0.7 all-gather.4.cloned.1.call-update
  7.3 0.0 all-gather.6.cloned.1.call-start
  7.3 1.0 multiply_exponential_fusion
  8.3 0.0 copy-start.2
  8.3 14.8 %fusion = bf16[2,4096,1024]{2,1,0:T(8,128)(2,1)} fusion(bf16[2,4096,1024]{2,1,0:T(8,128)(2,1)} %param.9, f32[2,32,1024]{2,1,0:T(8,128)S(1)} %multiply_exponential_fusion), kind=kLoop, calls=%fused_computation.1 | loop fusion | flops 25165824 | bytes 33816576 | tf_op jit(solution)/shard_map/convert_element_type | solution.py:38
  23.1 0.0 copy-done.2
  23.1 30.4 %all-gather.4.cloned.1.call-done = bf16[256,4096]{1,0:T(8,128)(2,1)} async-done(((bf16[16,4096]{1,0:T(8,128)(2,1)}), bf16[256,4096]{1,0:T(8,128)(2,1)}) %all-gather.4.cloned.1.call-update) | async-done | bytes 2097168 | tf_op jit(solution)/shard_map/all_gather | solution.py:49
  53.4 3.3 copy.8
  56.7 0.0 copy-start
  56.7 0.7 convert_multiply_fusion
  57.5 6.8 %fusion.11 = f32[256,64,64]{0,2,1:T(8,128)S(1)} fusion(f32[256,64,64]{0,2,1:T(8,128)S(1)} %bitcast.48), kind=kOutput, calls=%fused_computation.15 | convolution fusion | flops 805392384 | bytes 8388608 | tf_op jit(solution)/shard_map/ab,nbc,cd->nad/dot_general | solution.py:24
  64.2 6.0 %multiply_convert_fusion.1 = bf16[256,64,64]{0,2,1:T(8,128)(2,1)S(1)} fusion(f32[256,64,64]{0,2,1:T(8,128)S(1)} %fusion.11), kind=kOutput, calls=%fused_computation.17 | convolution fusion | flops 807489536 | bytes 6291456 | tf_op jit(solution)/shard_map/ab,nbc,cd->nad/dot_general | solution.py:24
  70.3 0.0 copy-done
  70.3 2.4 fusion.2
  72.6 0.0 copy-start.1
  72.6 2.4 fusion.20
  75.1 0.0 copy-done.1
  75.1 6.7 %fusion.5 = f32[256,1024]{1,0:T(8,128)} fusion(bf16[256,4096]{1,0:T(8,128)(2,1)S(1)} %copy-done.1, bf16[2,4096,1024]{2,1,0:T(8,128)(2,1)} %param.8), kind=kOutput, calls=%fused_computation.9 | convolution fusion | flops 2147483648 | bytes 11534336 | tf_op jit(solution)/shard_map/dot_general | solution.py:42
  81.8 12.7 %fusion.34 = f32[256,4096]{1,0:T(8,128)} fusion(bf16[1024,4096]{1,0:T(8,128)(2,1)} %param.11, bf16[256,4096]{1,0:T(8,128)(2,1)S(1)} %copy-done.1, bf16[2,4096,1024]{2,1,0:T(8,128)(2,1)} %param.8, bf16[256,1024]{1,0:T(8,128)(2,1)S(1)} %fusion.20, f32[256,1024]{1,0:T(8,128)} %fusion.5), kind=kOutput, calls=%fused_computation.27 | convolution fusion | flops 4297588736 | bytes 24641536 | tf_op jit(solution)/shard_map/dot_general | solution.py:54
  94.5 0.0 all-gather.6.cloned.1.call-update
  94.5 325.0 %all-gather.6.cloned.1.call-done = f32[4096,4096]{1,0:T(8,128)} async-done(((f32[256,4096]{1,0:T(8,128)}), f32[4096,4096]{1,0:T(8,128)}) %all-gather.6.cloned.1.call-update) | async-done | bytes 67108880 | tf_op jit(solution)/shard_map/all_gather | solution.py:55
  419.5 21.3 %reduce_sum.9 = bf16[256,4096]{1,0:T(8,128)(2,1)S(1)} reduce(f32[16,256,4096]{2,1,0:T(8,128)} %bitcast.9, f32[]{:T(128)} %constant.9.clone.1), dimensions={0}, to_apply=%region_0.1 | reduce | flops 15728640 | bytes 69206016 | tf_op jit(solution)/shard_map/reduce_sum | solution.py:55
  440.8 5.8 %multiply_convert_fusion = bf16[1024,4096]{1,0:T(8,128)(2,1)} fusion(bf16[256,1024]{1,0:T(8,128)(2,1)S(1)} %fusion.20, bf16[256,4096]{1,0:T(8,128)(2,1)S(1)} %reduce_sum.9), kind=kOutput, calls=%fused_computation.2 | convolution fusion | flops 2155872256 | bytes 11010048 | tf_op jit(solution)/shard_map/dot_general | solution.py:57
  (1 shorter events, 0.0 us)
Async XLA Ops:
  6.5 46.9 %all-gather.4.cloned.1.call-start = ((), (), s32[]{:S(2)}) async-start(), calls=%async_computation | async-start | bytes 2228224 | tf_op jit(solution)/shard_map/all_gather | solution.py:49
  7.3 412.2 %all-gather.6.cloned.1.call-start = ((), (), s32[]{:S(2)}) async-start(), calls=%async_computation.1 | async-start | bytes 71303168 | tf_op jit(solution)/shard_map/all_gather | solution.py:55
  8.3 14.8 %copy-start.2 = (s32[4096]{0:T(1024)S(1)}, s32[4096]{0:T(1024)}, u32[]{:S(2)}) copy-start(s32[4096]{0:T(1024)} %param.7) | copy-start | bytes 49156
  56.7 13.6 %copy-start = (bf16[2,4096,1024]{2,1,0:T(8,128)(2,1)S(1)}, bf16[2,4096,1024]{2,1,0:T(8,128)(2,1)}, u32[]{:S(2)}) copy-start(bf16[2,4096,1024]{2,1,0:T(8,128)(2,1)} %fusion) | copy-start | bytes 50331652
  72.6 2.5 copy-start.1
Sparse Core Ops, SparseCore 0:
  9.5 43.9 all-gather.3
  94.6 324.7 all-gather.5
